TPU v7x, 32 devices: a whole 2x2x4 slice. The times are simulated.
32 devices in a mesh: dp: 8 (over z, x), mp: 4 (over y, core).
Axes of the slice: x: 2, y: 2, z: 4, core: 2. Of those that a mesh axis runs over, the one named last changes fastest.
Arguments:
- hidden: bfloat16 [1280, 4096], P('mp', 'dp'), may hold values from -6 to 6
- qkv: bfloat16 [3, 1280, 4096], P(None, 'mp', 'dp'), may hold values from -18 to 18
- helper: int32 [64, 1], P('dp'), may hold values from 0 to 7; in each aligned block of 8 rows (0 to 7, 8 to 15, ...) no two rows name the same one
- segments: int32 [64, 64], P('dp'), may hold values from 0 to 1, as said below
- grad_attn: bfloat16 [1280, 4096], P('mp', 'dp'), may hold values from -6 to 6
Outputs:
- token_grads: bfloat16 [3, 1280, 4096], P(None, 'mp', 'dp')
- weight_grad: float32 [1280, 3, 1280], P('dp', None, 'mp')
Inputs may be any that keep to these rules, and one draw needn't show every extreme that they name: Among the 8 windows of one index of dp no helper is named more than 1 times, a bound that some block reaches. `segments`: within each slot the video number starts at 0 and steps at most once to 1, with 16 or more patches on each side of the step.
All inputs are finite; a program needn't handle non-finite values.
Results may differ from a plain program's by a relative error of at most 0.0095.
Values may be sent and summed in bfloat16 or wider, within the bound.
A program may use at most 64 MiB of HBM per device.

v0:
```python
import functools
import math

import jax
import jax.numpy as jnp
from jax import lax
from jax.experimental import pallas as pl
from jax.experimental.pallas import tpu as pltpu
from jax.sharding import PartitionSpec as P

HEAD_DIM = 80
MESH = pl.DeviceIdType.MESH


def contract(a, b, dims):
    return lax.dot_general(a, b, (dims, ((), ())), preferred_element_type=jnp.float32)


def pieces_of(total):
    lanes = 128
    sizes = [total % lanes] if total % lanes else []
    whole = total // lanes
    if whole > 3:
        sizes += [lanes] * whole
    else:
        sizes += [lanes] * whole
    out, high = [], total
    for size in sizes:
        high -= size
        out.append((high, size))
    return out


def shape_sent(rows, size):
    return (rows // 2, 2 * size) if 2 * size <= 128 and rows % 32 == 0 else (rows, size)


def kernel(n_dp, n_mp, helper_ref, hid_hbm, qkv_hbm, seg_ref, ga_hbm, tg_ref, wg_ref,
           hid_ref, qkv_ref, ga_ref, mate_tg,
           seg_send, seg_recv, ga_send, ga_recv, hid_all, prob_s, dout_s, acc, sends, recvs,
           load_sem, seg_ss, seg_rs, ga_ss, ga_rs, hx_ss, hx_rs, hy_ss, hy_rs, hp_ss, hp_rs, own_sem,
           tg_ss, tg_rs, st_ss, st_rs):
    d = lax.axis_index("dp")
    m = lax.axis_index("mp")
    y, c = m // 2, m % 2
    z, x = d // 2, d % 2
    far, groups = n_mp // 2, n_dp // 2
    win = seg_ref.shape[1]
    pair = 2 * win
    width, tokens = qkv_ref.shape[1], qkv_ref.shape[2]
    heads, pairs = width // HEAD_DIM, tokens // pair
    half = width // 2
    blocks, rows = hid_ref.shape[0], hid_ref.shape[2]
    scale = 1.0 / math.sqrt(HEAD_DIM)
    mate = 2 * y + 1 - c
    beside = 2 * z + 1 - x
    pieces = pieces_of(3 * width)
    bits = groups.bit_length() - 1
    bf16, f32 = jnp.bfloat16, jnp.float32

    barrier = pltpu.get_barrier_semaphore()
    for k in range(1, n_dp):
        pl.semaphore_signal(barrier, inc=1, device_id={"dp": lax.rem(d + k, n_dp)}, device_id_type=MESH)
    for k in range(1, far):
        pl.semaphore_signal(barrier, inc=1, device_id={"mp": 2 * lax.rem(y + k, far) + c}, device_id_type=MESH)
    pl.semaphore_signal(barrier, inc=1, device_id={"mp": mate}, device_id_type=MESH)

    loads = [pltpu.make_async_copy(a, b, load_sem.at[i])
             for i, (a, b) in enumerate(((ga_hbm, ga_ref), (hid_hbm, hid_ref), (qkv_hbm, qkv_ref)))]
    for load in loads:
        load.start()

    seg = seg_ref[...]
    seg_twice = jnp.concatenate([seg, seg], axis=1)
    for o in range(n_dp):
        seg_send[o] = seg_twice[o:o + 1]
    seg_recv[d] = seg_send[d]

    loads[0].wait()
    lane = lax.broadcasted_iota(jnp.int32, (half, pair), 1)
    low = lane < win
    for j in range(n_dp // 2):
        both = ga_ref[:, j * pair:(j + 1) * pair].astype(f32)
        top, bottom = both[:half], both[half:]
        ga_send[2 * j] = jnp.where(low, top, pltpu.roll(bottom, win, 1)).astype(bf16)
        ga_send[2 * j + 1] = jnp.where(low, pltpu.roll(top, win, 1), bottom).astype(bf16)
    ga_recv[d] = ga_send[d]
    loads[1].wait()

    def seg_copy(k):
        to = lax.rem(d + k, n_dp)
        return pltpu.make_async_remote_copy(seg_send.at[to], seg_recv.at[d], seg_ss.at[k], seg_rs.at[k],
                                            device_id={"dp": to}, device_id_type=MESH)

    def ga_copy(k):
        to = lax.rem(d + k, n_dp)
        return pltpu.make_async_remote_copy(ga_send.at[to], ga_recv.at[d], ga_ss.at[k], ga_rs.at[k],
                                            device_id={"dp": to}, device_id_type=MESH)

    def hid_at(side, member):
        return hid_all.at[side, pl.ds(member * blocks, blocks)]

    own = pltpu.make_async_copy(hid_ref.at[:, x], hid_at(0, m), own_sem)
    hid_x = pltpu.make_async_remote_copy(hid_ref.at[:, 1 - x], hid_at(1, m), hx_ss, hx_rs,
                                         device_id={"dp": beside}, device_id_type=MESH)

    def hid_copy(side, k):
        src = hid_ref.at[:, x] if side == 0 else hid_at(1, m)
        return pltpu.make_async_remote_copy(src, hid_at(side, m), hy_ss.at[side, k], hy_rs.at[side, k],
                                            device_id={"mp": 2 * lax.rem(y + k, far) + c}, device_id_type=MESH)

    def mate_copy(side, k):
        at = hid_at(side, 2 * lax.rem(y - k + far, far) + c)
        src = hid_ref.at[:, x] if (side, k) == (0, 0) else at
        return pltpu.make_async_remote_copy(src, at, hp_ss.at[side, k], hp_rs.at[side, k],
                                            device_id={"mp": mate}, device_id_type=MESH)

    pl.semaphore_wait(barrier, n_dp - 1 + far)
    for k in range(1, n_dp):
        seg_copy(k).start()
    for k in range(1, n_dp):
        ga_copy(k).start()
    hid_x.start()
    for k in range(1, far):
        hid_copy(0, k).start()
    mate_copy(0, 0).start()
    own.start()
    loads[2].wait()

    def at_of(p, h):
        return slice(h * HEAD_DIM, (h + 1) * HEAD_DIM), slice(p * pair, (p + 1) * pair)

    for p in range(pairs):
        for h in range(heads):
            at = at_of(p, h)
            prob_s[p * heads + h] = contract(qkv_ref[(1,) + at], qkv_ref[(0,) + at], ((0,), (0,))) * scale
    for k in range(1, n_dp):
        seg_copy(k).wait()
    lane_row = lax.broadcasted_iota(jnp.int32, (1, pair), 1)
    for p in range(pairs):
        first, second = seg_recv[helper_ref[2 * p]], seg_recv[helper_ref[2 * p + 1]]
        name = jnp.where(lane_row < win, first, second + 2).astype(f32)
        across = jnp.broadcast_to(name, (pair, pair))
        same = across == across.T
        for h in range(heads):
            scores = jnp.where(same, prob_s[p * heads + h], -1e30)
            prob = jnp.exp(scores - jnp.max(scores, axis=0, keepdims=True))
            prob_s[p * heads + h] = prob / jnp.sum(prob, axis=0, keepdims=True)

    for k in range(1, n_dp):
        ga_copy(k).wait()
    hid_x.wait()
    for k in range(1, far):
        hid_copy(1, k).start()
    mate_copy(1, 0).start()
    for k in range(1, far):
        hid_copy(0, k).wait()
        mate_copy(0, k).start()

    def tg_copy(s):
        at = pl.ds(*pieces[s])
        return pltpu.make_async_remote_copy(tg_ref.at[at], mate_tg.at[at], tg_ss.at[s], tg_rs.at[s],
                                            device_id={"dp": beside}, device_id_type=MESH)

    def put(j, p, h, grads):
        tg_ref[j * width + h * HEAD_DIM:j * width + (h + 1) * HEAD_DIM, p * pair:(p + 1) * pair] = grads.astype(bf16)

    for p in range(pairs):
        first = ga_recv[helper_ref[2 * p]].astype(f32)
        second = ga_recv[helper_ref[2 * p + 1]].astype(f32)
        top = jnp.where(low, first, pltpu.roll(second, win, 1))
        bottom = jnp.where(low, pltpu.roll(first, win, 1), second)
        dout_s[:, p * pair:(p + 1) * pair] = jnp.concatenate([top, bottom], axis=0).astype(bf16)
        for h in range(heads):
            put(2, p, h, contract(dout_s[at_of(p, h)], prob_s[p * heads + h].astype(bf16), ((1,), (1,))))
    early = [s for s, (start, _) in enumerate(pieces) if start >= 2 * width]
    for s in early:
        tg_copy(s).start()
    for p in range(pairs):
        for h in range(heads):
            at = at_of(p, h)
            query, key, value = qkv_ref[(0,) + at], qkv_ref[(1,) + at], qkv_ref[(2,) + at]
            prob = prob_s[p * heads + h]
            dprob = contract(value, dout_s[at], ((0,), (0,)))
            delta = jnp.sum(prob.astype(bf16).astype(f32) * dprob, axis=0, keepdims=True)
            dscore = (prob * (dprob - delta)).astype(bf16)
            put(0, p, h, contract(key, dscore, ((1,), (0,))) * scale)
            put(1, p, h, contract(query, dscore, ((1,), (1,))) * scale)
    for s in range(len(pieces)):
        if s not in early:
            tg_copy(s).start()

    own.wait()
    for k in range(1, far):
        hid_copy(1, k).wait()
        mate_copy(1, k).start()
    for side in range(2):
        for k in range(far):
            mate_copy(side, k).wait()

    def terms(s):
        at = slice(pieces[s][0], pieces[s][0] + pieces[s][1])
        if rows % 16 == 0:
            mine, theirs = [hid_all[side].reshape(groups * rows, tokens) for side in range(2)]
            sums = contract(mine, tg_ref[at], ((1,), (1,))) + contract(theirs, mate_tg[at], ((1,), (1,)))
            acc[s][...] = sums.reshape(groups, rows, pieces[s][1])
        else:
            for t in range(groups):
                acc[s][t] = (contract(hid_all[0, t], tg_ref[at], ((1,), (1,)))
                             + contract(hid_all[1, t], mate_tg[at], ((1,), (1,))))

    def half_copy(s, b):
        bit = z // 2 ** b % 2
        to = z + (1 - 2 * bit) * 2 ** b
        return pltpu.make_async_remote_copy(sends[s][b], recvs[s][b], st_ss.at[s, b], st_rs.at[s, b],
                                            device_id={"dp": 2 * to + x}, device_id_type=MESH)

    def begin(s, b):
        bit = z // 2 ** b % 2
        for i in range(groups >> (b + 1)):
            t = z % 2 ** b + (1 - bit) * 2 ** b + i * 2 ** (b + 1)
            block = acc[s][t]
            if sends[s][b].shape[1] != rows:
                block = jnp.concatenate([block[:rows // 2], block[rows // 2:]], axis=1)
            sends[s][b][i] = block.astype(bf16)
        half_copy(s, b).start()

    def end(s, b):
        half_copy(s, b).wait()
        bit = z // 2 ** b % 2
        for i in range(groups >> (b + 1)):
            t = z % 2 ** b + bit * 2 ** b + i * 2 ** (b + 1)
            block = recvs[s][b][i].astype(f32)
            if recvs[s][b].shape[1] != rows:
                block = jnp.concatenate([block[:, :pieces[s][1]], block[:, pieces[s][1]:]], axis=0)
            acc[s][t] = acc[s][t] + block

    def finish(s):
        start, size = pieces[s]
        total = acc[s][z]
        for j in range(3):
            a, b = max(start, j * width), min(start + size, (j + 1) * width)
            if a < b:
                wg_ref[j, :, a - j * width:b - j * width] = total[:, a - start:b - start]

    for turn in range(len(pieces) + 3 * bits):
        if turn < len(pieces):
            tg_copy(turn).wait()
            terms(turn)
            begin(turn, 0)
        for b in range(bits):
            s = turn - 2 - 3 * b
            if 0 <= s < len(pieces):
                end(s, b)
                if b + 1 < bits:
                    begin(s, b + 1)
                else:
                    finish(s)


def write_out(tg_ref, wg_ref, tg_hbm, wg_hbm, sems):
    copies = [pltpu.make_async_copy(tg_ref, tg_hbm, sems.at[0]), pltpu.make_async_copy(wg_ref, wg_hbm, sems.at[1])]
    for copy in copies:
        copy.start()
    for copy in copies:
        copy.wait()


def per_device(n_dp, n_mp, hidden, qkv, helper, segments, grad_attn):
    width, tokens = qkv.shape[1], qkv.shape[2]
    rows = hidden.shape[0] * n_mp // n_dp
    win = segments.shape[1]
    pair = 2 * win
    heads, pairs, groups, far = width // HEAD_DIM, tokens // pair, n_dp // 2, n_mp // 2
    bf16, f32 = jnp.bfloat16, jnp.float32
    vmem, anywhere = pl.BlockSpec(memory_space=pltpu.VMEM), pl.BlockSpec(memory_space=pltpu.HBM)
    dma = pltpu.SemaphoreType.DMA
    pieces = pieces_of(3 * width)
    bits = groups.bit_length() - 1
    halves = [[pltpu.VMEM((groups >> (b + 1),) + shape_sent(rows, size), bf16) for b in range(bits)] for _, size in pieces]
    split = hidden.reshape(-1, 2, rows, tokens)
    token_grads, weight_grad = pl.pallas_call(
        functools.partial(kernel, n_dp, n_mp),
        out_shape=(
            pltpu.VMEM((3 * width, tokens), bf16),
            pltpu.VMEM((3, rows, width), f32),
        ),
        in_specs=[pl.BlockSpec(memory_space=pltpu.SMEM), anywhere, anywhere, vmem, anywhere],
        out_specs=(vmem, vmem),
        scratch_shapes=[
            pltpu.VMEM(split.shape, bf16),
            pltpu.VMEM(qkv.shape, bf16),
            pltpu.VMEM(grad_attn.shape, bf16),
            pltpu.VMEM((3 * width, tokens), bf16),
            pltpu.VMEM((n_dp, 1, pair), jnp.int32),
            pltpu.VMEM((n_dp, 1, pair), jnp.int32),
            pltpu.VMEM((n_dp, width // 2, pair), bf16),
            pltpu.VMEM((n_dp, width // 2, pair), bf16),
            pltpu.VMEM((2, groups, rows, tokens), bf16),
            pltpu.VMEM((pairs * heads, pair, pair), f32),
            pltpu.VMEM((width, tokens), bf16),
            [pltpu.VMEM((groups, rows, size), f32) for _, size in pieces],
            halves,
            halves,
            dma((3,)),
            dma((n_dp,)), dma((n_dp,)), dma((n_dp,)), dma((n_dp,)),
            dma, dma, dma((2, far)), dma((2, far)), dma((2, far)), dma((2, far)), dma,
            dma((len(pieces),)), dma((len(pieces),)), dma((len(pieces), bits)), dma((len(pieces), bits)),
        ],
        compiler_params=pltpu.CompilerParams(
            collective_id=0, has_side_effects=True, vmem_limit_bytes=65000000
        ),
    )(helper[:, 0], split, qkv, segments, grad_attn)
    token_grads, weight_grad = pl.pallas_call(
        write_out,
        out_shape=(
            jax.ShapeDtypeStruct(token_grads.shape, bf16),
            jax.ShapeDtypeStruct(weight_grad.shape, f32),
        ),
        in_specs=[vmem, vmem],
        out_specs=(anywhere, anywhere),
        scratch_shapes=[dma((2,))],
        compiler_params=pltpu.CompilerParams(vmem_limit_bytes=8 * 1024 * 1024),
    )(token_grads, weight_grad)
    return token_grads.reshape(qkv.shape), jnp.transpose(weight_grad, (1, 0, 2))


def solution(mesh):
    in_specs = (P("mp", "dp"), P(None, "mp", "dp"), P("dp", None), P("dp", None), P("mp", "dp"))
    out_specs = (P(None, "mp", "dp"), P("dp", None, "mp"))
    return jax.shard_map(
        functools.partial(per_device, mesh.shape["dp"], mesh.shape["mp"]),
        mesh=mesh, in_specs=in_specs, out_specs=out_specs, check_vma=False,
    )
```

profile of v0, /device:TPU:0, one launch (start us, length us, event | category | flops | bytes accessed | tf_op | source)
XLA Modules:
  0.0 48.9 jit_solution(11290199961460800966)
XLA Ops:
  0.6 47.0 %shard_map.68 = (bf16[960,512]{1,0:T(8,128)(2,1)S(1)}, f32[3,160,320]{2,1,0:T(8,128)S(1)}) custom-call(s32[8]{0:T(128)} %bitcast.5, bf16[1,2,160,512]{3,2,1,0:T(8,128)(2,1)} %bitcast.4, bf16[3,320,512]{2,1,0:T(8,128)(2,1)} %qkv_hbm.1, s32[8,64]{1,0:T(8,128)} %seg_ref.1, bf16[320,512]{1,0:T(8,128)(2,1)} %ga_hbm.1), custom_call_target="tpu_custom_call" | custom-call | tf_op jit(solution)/shard_map/pallas_call | solution.py:282
  47.7 1.2 %shard_map.69 = (bf16[960,512]{1,0:T(8,128)(2,1)}, f32[3,160,320]{2,1,0:T(8,128)}) custom-call(bf16[960,512]{1,0:T(8,128)(2,1)S(1)} %get-tuple-element.6.tg_ref, f32[3,160,320]{2,1,0:T(8,128)S(1)} %get-tuple-element.7.wg_ref), custom_call_target="tpu_custom_call" | custom-call | tf_op jit(solution)/shard_map/pallas_call | solution.py:314
where the time goes:
time: 49.1 us; the launch traced here: 48.9 us
  Pallas kernels  48.2 us (98%)
  between operations  0.64 us (1%)
    pallas_call x1, Pallas kernels, per_device(): pl.pallas_call(functools.partial(kernel, n_dp, n_mp), out_shape=(pltpu.VM...  47 us
    pallas_call x1, Pallas kernels, per_device(): pl.pallas_call(write_out, out_shape=(jax.ShapeDtypeStruct(token_grads.sha...  1.21 us

commit v1 on v0

--- a/solution.py
+++ b/solution.py
@@ -35,8 +35,8 @@
     return (rows // 2, 2 * size) if 2 * size <= 128 and rows % 32 == 0 else (rows, size)
 
 
-def kernel(n_dp, n_mp, helper_ref, hid_hbm, qkv_hbm, seg_ref, ga_hbm, tg_ref, wg_ref,
-           hid_ref, qkv_ref, ga_ref, mate_tg,
+def kernel(n_dp, n_mp, helper_hbm, hid_hbm, qkv_hbm, seg_hbm, ga_hbm, tg_ref, wg_ref,
+           helper_ref, seg_ref, hid_ref, qkv_ref, ga_ref, mate_tg,
            seg_send, seg_recv, ga_send, ga_recv, hid_all, prob_s, dout_s, acc, sends, recvs,
            load_sem, seg_ss, seg_rs, ga_ss, ga_rs, hx_ss, hx_rs, hy_ss, hy_rs, hp_ss, hp_rs, own_sem,
            tg_ss, tg_rs, st_ss, st_rs):
@@ -58,23 +58,18 @@
     bits = groups.bit_length() - 1
     bf16, f32 = jnp.bfloat16, jnp.float32
 
+    loads = [pltpu.make_async_copy(a, b, load_sem.at[i])
+             for i, (a, b) in enumerate(((ga_hbm, ga_ref), (hid_hbm, hid_ref), (qkv_hbm, qkv_ref),
+                                         (seg_hbm, seg_ref), (helper_hbm, helper_ref)))]
+    for i in (0, 3, 1, 2, 4):
+        loads[i].start()
+
     barrier = pltpu.get_barrier_semaphore()
     for k in range(1, n_dp):
         pl.semaphore_signal(barrier, inc=1, device_id={"dp": lax.rem(d + k, n_dp)}, device_id_type=MESH)
     for k in range(1, far):
         pl.semaphore_signal(barrier, inc=1, device_id={"mp": 2 * lax.rem(y + k, far) + c}, device_id_type=MESH)
     pl.semaphore_signal(barrier, inc=1, device_id={"mp": mate}, device_id_type=MESH)
-
-    loads = [pltpu.make_async_copy(a, b, load_sem.at[i])
-             for i, (a, b) in enumerate(((ga_hbm, ga_ref), (hid_hbm, hid_ref), (qkv_hbm, qkv_ref)))]
-    for load in loads:
-        load.start()
-
-    seg = seg_ref[...]
-    seg_twice = jnp.concatenate([seg, seg], axis=1)
-    for o in range(n_dp):
-        seg_send[o] = seg_twice[o:o + 1]
-    seg_recv[d] = seg_send[d]
 
     loads[0].wait()
     lane = lax.broadcasted_iota(jnp.int32, (half, pair), 1)
@@ -85,6 +80,12 @@
         ga_send[2 * j] = jnp.where(low, top, pltpu.roll(bottom, win, 1)).astype(bf16)
         ga_send[2 * j + 1] = jnp.where(low, pltpu.roll(top, win, 1), bottom).astype(bf16)
     ga_recv[d] = ga_send[d]
+    loads[3].wait()
+    seg = seg_ref[...]
+    seg_twice = jnp.concatenate([seg, seg], axis=1)
+    for o in range(n_dp):
+        seg_send[o] = seg_twice[o:o + 1]
+    seg_recv[d] = seg_send[d]
     loads[1].wait()
 
     def seg_copy(k):
@@ -118,14 +119,17 @@
     pl.semaphore_wait(barrier, n_dp - 1 + far)
     for k in range(1, n_dp):
         seg_copy(k).start()
-    for k in range(1, n_dp):
+    for k in range(2, n_dp, 2):
         ga_copy(k).start()
     hid_x.start()
+    for k in range(1, n_dp, 2):
+        ga_copy(k).start()
     for k in range(1, far):
         hid_copy(0, k).start()
     mate_copy(0, 0).start()
     own.start()
     loads[2].wait()
+    loads[4].wait()
 
     def at_of(p, h):
         return slice(h * HEAD_DIM, (h + 1) * HEAD_DIM), slice(p * pair, (p + 1) * pair)
@@ -147,8 +151,6 @@
             prob = jnp.exp(scores - jnp.max(scores, axis=0, keepdims=True))
             prob_s[p * heads + h] = prob / jnp.sum(prob, axis=0, keepdims=True)
 
-    for k in range(1, n_dp):
-        ga_copy(k).wait()
     hid_x.wait()
     for k in range(1, far):
         hid_copy(1, k).start()
@@ -156,6 +158,8 @@
     for k in range(1, far):
         hid_copy(0, k).wait()
         mate_copy(0, k).start()
+    for k in range(1, n_dp):
+        ga_copy(k).wait()
 
     def tg_copy(s):
         at = pl.ds(*pieces[s])
@@ -177,6 +181,10 @@
     for s in early:
         tg_copy(s).start()
     for p in range(pairs):
+        if p == pairs // 2:
+            for k in range(1, far):
+                hid_copy(1, k).wait()
+                mate_copy(1, k).start()
         for h in range(heads):
             at = at_of(p, h)
             query, key, value = qkv_ref[(0,) + at], qkv_ref[(1,) + at], qkv_ref[(2,) + at]
@@ -191,9 +199,6 @@
             tg_copy(s).start()
 
     own.wait()
-    for k in range(1, far):
-        hid_copy(1, k).wait()
-        mate_copy(1, k).start()
     for side in range(2):
         for k in range(far):
             mate_copy(side, k).wait()
@@ -285,9 +290,11 @@
             pltpu.VMEM((3 * width, tokens), bf16),
             pltpu.VMEM((3, rows, width), f32),
         ),
-        in_specs=[pl.BlockSpec(memory_space=pltpu.SMEM), anywhere, anywhere, vmem, anywhere],
+        in_specs=[anywhere] * 5,
         out_specs=(vmem, vmem),
         scratch_shapes=[
+            pltpu.SMEM(helper.shape[:1], jnp.int32),
+            pltpu.VMEM(segments.shape, jnp.int32),
             pltpu.VMEM(split.shape, bf16),
             pltpu.VMEM(qkv.shape, bf16),
             pltpu.VMEM(grad_attn.shape, bf16),
@@ -302,7 +309,7 @@
             [pltpu.VMEM((groups, rows, size), f32) for _, size in pieces],
             halves,
             halves,
-            dma((3,)),
+            dma((5,)),
             dma((n_dp,)), dma((n_dp,)), dma((n_dp,)), dma((n_dp,)),
             dma, dma, dma((2, far)), dma((2, far)), dma((2, far)), dma((2, far)), dma,
             dma((len(pieces),)), dma((len(pieces),)), dma((len(pieces), bits)), dma((len(pieces), bits)),

time: 49.1 us -> 48.4 us (0.986)
  Pallas kernels: 48.2 us -> 47.6 us
    pallas_call x1, Pallas kernels: 47 us -> 46.4 us  [per_device(): pl.pallas_call(functools.partial(kernel, n_dp, n_mp), out_shape=(pltpu.VM...]
where the time goes in v1:
time: 48.4 us; the launch traced here: 48.2 us
  Pallas kernels  47.6 us (98%)
  between operations  0.64 us (1%)
    pallas_call x1, Pallas kernels, per_device(): pl.pallas_call(functools.partial(kernel, n_dp, n_mp), out_shape=(pltpu.VM...  46.4 us
    pallas_call x1, Pallas kernels, per_device(): pl.pallas_call(write_out, out_shape=(jax.ShapeDtypeStruct(token_grads.sha...  1.21 us

profile of v1, /device:TPU:0, one launch (start us, length us, event | category | flops | bytes accessed | tf_op | source)
XLA Modules:
  0.0 48.2 jit_solution(14093157512111042250)
XLA Ops:
  0.6 46.4 %shard_map.68 = (bf16[960,512]{1,0:T(8,128)(2,1)S(1)}, f32[3,160,320]{2,1,0:T(8,128)S(1)}) custom-call(s32[8]{0:T(128)} %bitcast.5, bf16[1,2,160,512]{3,2,1,0:T(8,128)(2,1)} %bitcast.4, bf16[3,320,512]{2,1,0:T(8,128)(2,1)} %qkv_hbm.1, s32[8,64]{1,0:T(8,128)} %seg_hbm.1, bf16[320,512]{1,0:T(8,128)(2,1)} %ga_hbm.1), custom_call_target="tpu_custom_call" | custom-call | tf_op jit(solution)/shard_map/pallas_call | solution.py:287
  47.0 1.2 %shard_map.69 = (bf16[960,512]{1,0:T(8,128)(2,1)}, f32[3,160,320]{2,1,0:T(8,128)}) custom-call(bf16[960,512]{1,0:T(8,128)(2,1)S(1)} %get-tuple-element.6.tg_ref, f32[3,160,320]{2,1,0:T(8,128)S(1)} %get-tuple-element.7.wg_ref), custom_call_target="tpu_custom_call" | custom-call | tf_op jit(solution)/shard_map/pallas_call | solution.py:321

commit v2 on v1

v2 whole, which is shorter than its diff:
```python
import functools
import math

import jax
import jax.numpy as jnp
from jax import lax
from jax.experimental import pallas as pl
from jax.experimental.pallas import tpu as pltpu
from jax.sharding import PartitionSpec as P

HEAD_DIM = 80
DIRECT_PIECES = 1
MESH = pl.DeviceIdType.MESH


def contract(a, b, dims):
    return lax.dot_general(a, b, (dims, ((), ())), preferred_element_type=jnp.float32)


def parts_of(width):
    return 2 if width // HEAD_DIM % 2 == 0 and width >= 256 else 1


def pieces_of(width):
    lanes, parts = 128, parts_of(width)
    if parts == 1:
        sizes = [3 * width % lanes] * (3 * width % lanes > 0) + [lanes] * (3 * width // lanes)
        out, high = [], 3 * width
        for size in sizes:
            high -= size
            out.append((high, size))
        return out
    upper, lower = [], []
    for j in (2, 1, 0):
        high = (j + 1) * width
        for i in range(width // parts // lanes):
            high -= lanes
            upper += [(high + lanes // 2, lanes // 2), (high, lanes // 2)] if j == 2 and i == 0 else [(high, lanes)]
        while high > j * width:
            size = min(lanes, high - j * width)
            high -= size
            lower.append((high, size))
    return upper + lower


def halved(pieces, parts):
    return pieces[:len(pieces) - DIRECT_PIECES] if parts > 1 else pieces


def shape_sent(rows, size):
    return (rows // 2, 2 * size) if 2 * size <= 128 and rows % 32 == 0 else (rows, size)


def kernel(n_dp, n_mp, helper_hbm, hid_hbm, qkv_hbm, seg_hbm, ga_hbm, tg_ref, wg_ref,
           helper_ref, seg_ref, hid_ref, qkv_ref, ga_ref, mate_tg,
           seg_send, seg_recv, ga_send, ga_recv, hid_all, prob_s, dout_s, acc, sends, recvs, straight_out, straight_in,
           load_sem, seg_ss, seg_rs, ga_ss, ga_rs, hx_ss, hx_rs, hz_ss, hz_rs, hy_ss, hy_rs, hp_ss, hp_rs, own_sem,
           tg_ss, tg_rs, st_ss, st_rs, di_ss, di_rs):
    d = lax.axis_index("dp")
    m = lax.axis_index("mp")
    y, c = m // 2, m % 2
    z, x = d // 2, d % 2
    far, groups = n_mp // 2, n_dp // 2
    win = seg_ref.shape[1]
    pair = 2 * win
    width, tokens = qkv_ref.shape[1], qkv_ref.shape[2]
    heads, pairs = width // HEAD_DIM, tokens // pair
    parts = parts_of(width)
    band = width // parts
    half = band // 2
    blocks, rows = hid_ref.shape[0], hid_ref.shape[2]
    scale = 1.0 / math.sqrt(HEAD_DIM)
    mate = 2 * y + 1 - c
    beside = 2 * z + 1 - x
    pieces = pieces_of(width)
    bits = groups.bit_length() - 1
    bf16, f32 = jnp.bfloat16, jnp.float32

    loads = [pltpu.make_async_copy(a, b, load_sem.at[i])
             for i, (a, b) in enumerate(((ga_hbm, ga_ref), (hid_hbm, hid_ref), (qkv_hbm, qkv_ref),
                                         (seg_hbm, seg_ref), (helper_hbm, helper_ref)))]
    for i in (0, 3, 1, 2, 4):
        loads[i].start()

    barrier = pltpu.get_barrier_semaphore()
    for k in range(1, n_dp):
        pl.semaphore_signal(barrier, inc=1, device_id={"dp": lax.rem(d + k, n_dp)}, device_id_type=MESH)
    for k in range(1, far):
        pl.semaphore_signal(barrier, inc=1, device_id={"mp": 2 * lax.rem(y + k, far) + c}, device_id_type=MESH)
    pl.semaphore_signal(barrier, inc=1, device_id={"mp": mate}, device_id_type=MESH)

    loads[0].wait()
    lane = lax.broadcasted_iota(jnp.int32, (half, pair), 1)
    low = lane < win
    for j in range(n_dp // 2):
        both = ga_ref[:, j * pair:(j + 1) * pair].astype(f32)
        for g in range(parts):
            top, bottom = both[g * band:g * band + half], both[g * band + half:(g + 1) * band]
            ga_send[g, 2 * j] = jnp.where(low, top, pltpu.roll(bottom, win, 1)).astype(bf16)
            ga_send[g, 2 * j + 1] = jnp.where(low, pltpu.roll(top, win, 1), bottom).astype(bf16)
    for g in range(parts):
        ga_recv[g][d] = ga_send[g, d]
    loads[3].wait()
    seg = seg_ref[...]
    seg_twice = jnp.concatenate([seg, seg], axis=1)
    for o in range(n_dp):
        seg_send[o] = seg_twice[o:o + 1]
    seg_recv[d] = seg_send[d]
    loads[1].wait()

    def seg_copy(k):
        to = lax.rem(d + k, n_dp)
        return pltpu.make_async_remote_copy(seg_send.at[to], seg_recv.at[d], seg_ss, seg_rs,
                                            device_id={"dp": to}, device_id_type=MESH)

    others = pl.ds(0, n_dp - 1)
    seg_all = pltpu.make_async_remote_copy(seg_send.at[others], seg_recv.at[others], seg_ss, seg_rs,
                                           device_id={"dp": beside}, device_id_type=MESH)

    def ga_copy(g, k):
        to = lax.rem(d + k, n_dp)
        return pltpu.make_async_remote_copy(ga_send.at[g, to], ga_recv[g].at[d], ga_ss.at[g], ga_rs.at[g],
                                            device_id={"dp": to}, device_id_type=MESH)

    def ga_all(g):
        return pltpu.make_async_remote_copy(ga_send.at[g, others], ga_recv[g].at[others], ga_ss.at[g], ga_rs.at[g],
                                            device_id={"dp": beside}, device_id_type=MESH)

    def hid_at(side, member):
        return hid_all.at[side, pl.ds(member * blocks, blocks)]

    own = pltpu.make_async_copy(hid_ref.at[:, x], hid_at(0, m), own_sem)
    chunks = 5 if rows % 80 == 0 else 1

    def hid_x(q):
        at = pl.ds(q * (rows // chunks), rows // chunks)
        return pltpu.make_async_remote_copy(hid_ref.at[:, 1 - x, at], hid_at(1, m).at[:, at], hx_ss, hx_rs.at[q],
                                            device_id={"dp": beside}, device_id_type=MESH)

    def pass_copy(q, k):
        at = pl.ds(q * (rows // chunks), rows // chunks)
        return pltpu.make_async_remote_copy(hid_at(1, m).at[:, at], hid_at(1, m).at[:, at], hz_ss, hz_rs,
                                            device_id={"mp": 2 * lax.rem(y + k, far) + c}, device_id_type=MESH)

    def hid_copy(k):
        return pltpu.make_async_remote_copy(hid_ref.at[:, x], hid_at(0, m), hy_ss, hy_rs,
                                            device_id={"mp": 2 * lax.rem(y + k, far) + c}, device_id_type=MESH)

    def mate_copy(side, k):
        at = hid_at(side, 2 * lax.rem(y - k + far, far) + c)
        src = hid_ref.at[:, x] if (side, k) == (0, 0) else at
        return pltpu.make_async_remote_copy(src, at, hp_ss.at[side], hp_rs.at[side],
                                            device_id={"mp": mate}, device_id_type=MESH)

    def members(side, count, send, recv):
        at = hid_all.at[side, pl.ds(0, count * blocks)]
        return pltpu.make_async_remote_copy(at, at, send, recv, device_id={"mp": mate}, device_id_type=MESH)

    pl.semaphore_wait(barrier, n_dp - 1 + far)
    for k in range(1, n_dp):
        seg_copy(k).start()
    for k in range(1, far):
        hid_copy(k).start()
    for g in reversed(range(parts)):
        for k in range(1, n_dp):
            ga_copy(g, k).start()
        if g == parts - 1:
            for q in range(chunks):
                hid_x(q).start()
    mate_copy(0, 0).start()
    own.start()
    loads[2].wait()
    loads[4].wait()

    def at_of(p, h):
        return slice(h * HEAD_DIM, (h + 1) * HEAD_DIM), slice(p * pair, (p + 1) * pair)

    for p in range(pairs):
        for h in range(heads):
            at = at_of(p, h)
            prob_s[p * heads + h] = contract(qkv_ref[(1,) + at], qkv_ref[(0,) + at], ((0,), (0,))) * scale
    seg_all.wait()
    lane_row = lax.broadcasted_iota(jnp.int32, (1, pair), 1)
    for p in range(pairs):
        first, second = seg_recv[helper_ref[2 * p]], seg_recv[helper_ref[2 * p + 1]]
        name = jnp.where(lane_row < win, first, second + 2).astype(f32)
        across = jnp.broadcast_to(name, (pair, pair))
        same = across == across.T
        for h in range(heads):
            scores = jnp.where(same, prob_s[p * heads + h], -1e30)
            prob = jnp.exp(scores - jnp.max(scores, axis=0, keepdims=True))
            prob_s[p * heads + h] = prob / jnp.sum(prob, axis=0, keepdims=True)

    def pass_on(q):
        hid_x(q).wait_recv()
        for k in range(1, far):
            pass_copy(q, k).start()

    before = min(2, chunks)
    for q in range(before):
        pass_on(q)

    def tg_copy(s):
        at = pl.ds(*pieces[s])
        return pltpu.make_async_remote_copy(tg_ref.at[at], mate_tg.at[at], tg_ss, tg_rs.at[s],
                                            device_id={"dp": beside}, device_id_type=MESH)

    def put(j, p, h, grads):
        tg_ref[j * width + h * HEAD_DIM:j * width + (h + 1) * HEAD_DIM, p * pair:(p + 1) * pair] = grads.astype(bf16)

    def dv(g, p):
        first = ga_recv[g][helper_ref[2 * p]].astype(f32)
        second = ga_recv[g][helper_ref[2 * p + 1]].astype(f32)
        top = jnp.where(low, first, pltpu.roll(second, win, 1))
        bottom = jnp.where(low, pltpu.roll(first, win, 1), second)
        dout_s[g * band:(g + 1) * band, p * pair:(p + 1) * pair] = jnp.concatenate([top, bottom], axis=0).astype(bf16)
        for h in range(g * heads // parts, (g + 1) * heads // parts):
            put(2, p, h, contract(dout_s[at_of(p, h)], prob_s[p * heads + h].astype(bf16), ((1,), (1,))))

    def attend(g, p):
        for h in range(g * heads // parts, (g + 1) * heads // parts):
            at = at_of(p, h)
            query, key, value = qkv_ref[(0,) + at], qkv_ref[(1,) + at], qkv_ref[(2,) + at]
            prob = prob_s[p * heads + h]
            dprob = contract(value, dout_s[at], ((0,), (0,)))
            delta = jnp.sum(prob.astype(bf16).astype(f32) * dprob, axis=0, keepdims=True)
            dscore = (prob * (dprob - delta)).astype(bf16)
            put(0, p, h, contract(key, dscore, ((1,), (0,))) * scale)
            put(1, p, h, contract(query, dscore, ((1,), (1,))) * scale)

    sent = []

    def send_ready(g, j):
        for s, (start, size) in enumerate(pieces):
            if s not in sent and start // width >= j and (start % width >= g * band or parts == 1 or g == 0):
                if start // width == 2 or j < 2:
                    tg_copy(s).start()
                    sent.append(s)

    later = max(before, chunks - 1)
    for g in reversed(range(parts)):
        ga_all(g).wait()
        for p in range(pairs):
            dv(g, p)
        send_ready(g, 2)
        if g == parts - 1:
            for q in range(before, later):
                pass_on(q)
            members(0, far - 1, hy_ss, hy_rs).wait()
            for k in range(1, far):
                mate_copy(0, k).start()
        for p in range(pairs if g > 0 else 0):
            if p == 1:
                for q in range(later, chunks):
                    pass_on(q)
                mate_copy(1, 0).start()
            attend(g, p)
        if g > 0:
            send_ready(g, 0)
    if parts == 1:
        mate_copy(1, 0).start()
    members(1, far - 1, hz_ss, hz_rs).wait()
    for k in range(1, far):
        mate_copy(1, k).start()
    own.wait()
    members(0, far, hp_ss.at[0], hp_rs.at[0]).wait()

    def products(side, of, s, blocks):
        at = slice(pieces[s][0], pieces[s][0] + pieces[s][1])
        if rows % 16 == 0:
            stacked = jnp.concatenate([hid_all[side, t] for t in blocks], axis=0)
            return contract(stacked, of[at], ((1,), (1,))).reshape(len(blocks), rows, pieces[s][1])
        return [contract(hid_all[side, t], of[at], ((1,), (1,))) for t in blocks]

    def mine(s):
        for t, block in enumerate(products(0, tg_ref, s, range(groups))):
            acc[s][t] = block

    def theirs(s, blocks):
        for t, block in zip(blocks, products(1, mate_tg, s, blocks)):
            acc[s][t] = acc[s][t] + block

    def packed(block):
        if block.shape[1] * 2 <= 128 and rows % 32 == 0:
            block = jnp.concatenate([block[:rows // 2], block[rows // 2:]], axis=1)
        return block.astype(bf16)

    def unpacked(block, size):
        block = block.astype(f32)
        if block.shape[1] != size:
            block = jnp.concatenate([block[:, :size], block[:, size:]], axis=0)
        return block

    def finish(s, total):
        start, size = pieces[s]
        for j in range(3):
            a, b = max(start, j * width), min(start + size, (j + 1) * width)
            if a < b:
                wg_ref[j, :, a - j * width:b - j * width] = total[:, a - start:b - start]

    count = len(pieces)
    straight = len(halved(pieces, parts))
    kinds = sorted({size for _, size in pieces[:straight]})
    place = [(kinds.index(size), sum(other == size for _, other in pieces[:s])) for s, (_, size) in enumerate(pieces[:straight])]

    def outgoing(s, b):
        kind, at = place[s]
        return sends[kind][b].at[at]

    def half_copy(s, b):
        bit = z // 2 ** b % 2
        to = z + (1 - 2 * bit) * 2 ** b
        return pltpu.make_async_remote_copy(outgoing(s, b), recvs[s][b], st_ss.at[place[s][0], b], st_rs.at[s, b],
                                            device_id={"dp": 2 * to + x}, device_id_type=MESH)

    def begin(s, b):
        bit = z // 2 ** b % 2
        for i in range(groups >> (b + 1)):
            t = z % 2 ** b + (1 - bit) * 2 ** b + i * 2 ** (b + 1)
            outgoing(s, b)[i] = packed(acc[s][t])
        half_copy(s, b).start()

    def end(s, b):
        half_copy(s, b).wait_recv()
        bit = z // 2 ** b % 2
        for i in range(groups >> (b + 1)):
            t = z % 2 ** b + bit * 2 ** b + i * 2 ** (b + 1)
            acc[s][t] = acc[s][t] + unpacked(recvs[s][b][i], pieces[s][1])

    def direct_copy(s, k):
        return pltpu.make_async_remote_copy(straight_out.at[s, k - 1], straight_in.at[s, k - 1], di_ss, di_rs,
                                            device_id={"dp": 2 * lax.rem(z + k, groups) + x}, device_id_type=MESH)

    ahead = 2 if parts > 1 else 0
    attends = {2: range(pairs // 2), 3: range(pairs // 2, pairs)} if parts > 1 else {0: range(pairs)}
    for s in range(ahead):
        mine(s)
    members(1, far, hp_ss.at[1], hp_rs.at[1]).wait()
    bit = z % 2
    sent_first = [1 - bit + 2 * i for i in range(groups // 2)]
    kept = [bit + 2 * i for i in range(groups // 2)]
    for turn in range(count + 2 + 4 * (bits - 1)):
        for p in attends.get(turn, ()):
            attend(0, p)
        if turn == max(attends):
            send_ready(0, 0)
        if turn < count:
            if turn >= ahead:
                mine(turn)
            tg_copy(turn).wait_recv()
            if turn < straight:
                theirs(turn, sent_first)
                begin(turn, 0)
                theirs(turn, kept)
            else:
                theirs(turn, range(groups))
                for k in range(1, groups):
                    straight_out[turn - straight, k - 1] = packed(acc[turn][lax.rem(z + k, groups)])
                    direct_copy(turn - straight, k).start()
        for b in range(bits):
            s = turn - 2 - 4 * b
            if 0 <= s < straight:
                end(s, b)
                if b + 1 < bits:
                    begin(s, b + 1)
                else:
                    finish(s, acc[s][z])
    if straight < count:
        pltpu.make_async_remote_copy(straight_out, straight_in, di_ss, di_rs,
                                     device_id={"dp": beside}, device_id_type=MESH).wait()
    for s in range(straight, count):
        total = acc[s][z]
        for k in range(1, groups):
            total = total + unpacked(straight_in[s - straight, k - 1], pieces[s][1])
        finish(s, total)
    pltpu.make_async_remote_copy(tg_ref, mate_tg, tg_ss, tg_rs.at[0],
                                 device_id={"dp": beside}, device_id_type=MESH).wait_send()
    pltpu.make_async_remote_copy(hid_ref.at[:, 1 - x], hid_at(1, m), hx_ss, hx_rs.at[0],
                                 device_id={"dp": beside}, device_id_type=MESH).wait_send()
    for kind in range(len(kinds)):
        for b in range(bits):
            pltpu.make_async_remote_copy(sends[kind][b], sends[kind][b], st_ss.at[kind, b], st_rs.at[0, b],
                                         device_id={"dp": beside}, device_id_type=MESH).wait_send()


def write_out(tg_ref, wg_ref, tg_hbm, wg_hbm, sems):
    copies = [pltpu.make_async_copy(tg_ref, tg_hbm, sems.at[0]), pltpu.make_async_copy(wg_ref, wg_hbm, sems.at[1])]
    for copy in copies:
        copy.start()
    for copy in copies:
        copy.wait()


def per_device(n_dp, n_mp, hidden, qkv, helper, segments, grad_attn):
    width, tokens = qkv.shape[1], qkv.shape[2]
    rows = hidden.shape[0] * n_mp // n_dp
    win = segments.shape[1]
    pair = 2 * win
    parts = parts_of(width)
    heads, pairs, groups, far = width // HEAD_DIM, tokens // pair, n_dp // 2, n_mp // 2
    bf16, f32 = jnp.bfloat16, jnp.float32
    vmem, anywhere = pl.BlockSpec(memory_space=pltpu.VMEM), pl.BlockSpec(memory_space=pltpu.HBM)
    dma = pltpu.SemaphoreType.DMA
    pieces = pieces_of(width)
    bits = groups.bit_length() - 1
    cut = halved(pieces, parts)
    incoming = [[pltpu.VMEM((groups >> (b + 1),) + shape_sent(rows, size), bf16) for b in range(bits)] for _, size in cut]
    kinds = sorted({size for _, size in cut})
    outgoing = [[pltpu.VMEM((sum(size == kind for _, size in cut), groups >> (b + 1)) + shape_sent(rows, kind), bf16)
                 for b in range(bits)] for kind in kinds]
    straight = pltpu.VMEM((max(len(pieces) - len(cut), 1), groups - 1) + shape_sent(rows, pieces[-1][1]), bf16)
    split = hidden.reshape(-1, 2, rows, tokens)
    token_grads, weight_grad = pl.pallas_call(
        functools.partial(kernel, n_dp, n_mp),
        out_shape=(
            pltpu.VMEM((3 * width, tokens), bf16),
            pltpu.VMEM((3, rows, width), f32),
        ),
        in_specs=[anywhere] * 5,
        out_specs=(vmem, vmem),
        scratch_shapes=[
            pltpu.SMEM(helper.shape[:1], jnp.int32),
            pltpu.VMEM(segments.shape, jnp.int32),
            pltpu.VMEM(split.shape, bf16),
            pltpu.VMEM(qkv.shape, bf16),
            pltpu.VMEM(grad_attn.shape, bf16),
            pltpu.VMEM((3 * width, tokens), bf16),
            pltpu.VMEM((n_dp, 1, pair), jnp.int32),
            pltpu.VMEM((n_dp, 1, pair), jnp.int32),
            pltpu.VMEM((parts, n_dp, width // parts // 2, pair), bf16),
            [pltpu.VMEM((n_dp, width // parts // 2, pair), bf16) for _ in range(parts)],
            pltpu.VMEM((2, groups, rows, tokens), bf16),
            pltpu.VMEM((pairs * heads, pair, pair), f32),
            pltpu.VMEM((width, tokens), bf16),
            [pltpu.VMEM((groups, rows, size), f32) for _, size in pieces],
            outgoing,
            incoming,
            straight,
            straight,
            dma((5,)),
            dma, dma, dma((parts,)), dma((parts,)),
            dma, dma((5 if rows % 80 == 0 else 1,)), dma, dma, dma, dma, dma((2,)), dma((2,)), dma,
            dma, dma((len(pieces),)), dma((len(kinds), bits)), dma((len(cut), bits)),
            dma, dma,
        ],
        compiler_params=pltpu.CompilerParams(
            collective_id=0, has_side_effects=True, vmem_limit_bytes=65000000
        ),
    )(helper[:, 0], split, qkv, segments, grad_attn)
    token_grads, weight_grad = pl.pallas_call(
        write_out,
        out_shape=(
            jax.ShapeDtypeStruct(token_grads.shape, bf16),
            jax.ShapeDtypeStruct(weight_grad.shape, f32),
        ),
        in_specs=[vmem, vmem],
        out_specs=(anywhere, anywhere),
        scratch_shapes=[dma((2,))],
        compiler_params=pltpu.CompilerParams(vmem_limit_bytes=8 * 1024 * 1024),
    )(token_grads, weight_grad)
    return token_grads.reshape(qkv.shape), jnp.transpose(weight_grad, (1, 0, 2))


def solution(mesh):
    in_specs = (P("mp", "dp"), P(None, "mp", "dp"), P("dp", None), P("dp", None), P("mp", "dp"))
    out_specs = (P(None, "mp", "dp"), P("dp", None, "mp"))
    return jax.shard_map(
        functools.partial(per_device, mesh.shape["dp"], mesh.shape["mp"]),
        mesh=mesh, in_specs=in_specs, out_specs=out_specs, check_vma=False,
    )
```

time: 48.4 us -> 45.6 us (0.942)
  Pallas kernels: 47.6 us -> 44.8 us
    pallas_call x1, Pallas kernels: 46.4 us -> 43.6 us  [per_device(): pl.pallas_call(functools.partial(kernel, n_dp, n_mp), out_shape=(pltpu.VM...]
where the time goes in v2:
time: 45.6 us; the launch traced here: 45.4 us
  Pallas kernels  44.8 us (98%)
  between operations  0.64 us (1%)
    pallas_call x1, Pallas kernels, per_device(): pl.pallas_call(functools.partial(kernel, n_dp, n_mp), out_shape=(pltpu.VM...  43.6 us
    pallas_call x1, Pallas kernels, per_device(): pl.pallas_call(write_out, out_shape=(jax.ShapeDtypeStruct(token_grads.sha...  1.21 us

profile of v2, /device:TPU:0, one launch (start us, length us, event | category | flops | bytes accessed | tf_op | source)
XLA Modules:
  0.0 45.4 jit_solution(6756827478363189251)
XLA Ops:
  0.6 43.6 %shard_map.68 = (bf16[960,512]{1,0:T(8,128)(2,1)S(1)}, f32[3,160,320]{2,1,0:T(8,128)S(1)}) custom-call(s32[8]{0:T(128)} %bitcast.5, bf16[1,2,160,512]{3,2,1,0:T(8,128)(2,1)} %bitcast.4, bf16[3,320,512]{2,1,0:T(8,128)(2,1)} %qkv_hbm.1, s32[8,64]{1,0:T(8,128)} %seg_hbm.1, bf16[320,512]{1,0:T(8,128)(2,1)} %ga_hbm.1), custom_call_target="tpu_custom_call" | custom-call | tf_op jit(solution)/shard_map/pallas_call | solution.py:413
  44.2 1.2 %shard_map.69 = (bf16[960,512]{1,0:T(8,128)(2,1)}, f32[3,160,320]{2,1,0:T(8,128)}) custom-call(bf16[960,512]{1,0:T(8,128)(2,1)S(1)} %get-tuple-element.6.tg_ref, f32[3,160,320]{2,1,0:T(8,128)S(1)} %get-tuple-element.7.wg_ref), custom_call_target="tpu_custom_call" | custom-call | tf_op jit(solution)/shard_map/pallas_call | solution.py:450

commit v3 on v2

--- a/solution.py
+++ b/solution.py
@@ -161,12 +161,10 @@
         seg_copy(k).start()
     for k in range(1, far):
         hid_copy(k).start()
-    for g in reversed(range(parts)):
-        for k in range(1, n_dp):
-            ga_copy(g, k).start()
-        if g == parts - 1:
-            for q in range(chunks):
-                hid_x(q).start()
+    for k in range(1, n_dp):
+        ga_copy(parts - 1, k).start()
+    for q in range(chunks):
+        hid_x(q).start()
     mate_copy(0, 0).start()
     own.start()
     loads[2].wait()
@@ -197,6 +195,9 @@
             pass_copy(q, k).start()
 
     before = min(2, chunks)
+    for g in range(parts - 1):
+        for k in range(1, n_dp):
+            ga_copy(g, k).start()
     for q in range(before):
         pass_on(q)
 
@@ -331,6 +332,16 @@
         return pltpu.make_async_remote_copy(straight_out.at[s, k - 1], straight_in.at[s, k - 1], di_ss, di_rs,
                                             device_id={"dp": 2 * lax.rem(z + k, groups) + x}, device_id_type=MESH)
 
+    def advance(s, b):
+        if 0 <= s < straight:
+            end(s, b)
+            if b + 1 < bits:
+                begin(s, b + 1)
+            else:
+                finish(s, acc[s][z])
+
+    swapped = groups == 4
+    inner = z == 2
     ahead = 2 if parts > 1 else 0
     attends = {2: range(pairs // 2), 3: range(pairs // 2, pairs)} if parts > 1 else {0: range(pairs)}
     for s in range(ahead):
@@ -350,21 +361,23 @@
             tg_copy(turn).wait_recv()
             if turn < straight:
                 theirs(turn, sent_first)
+                if swapped:
+                    pl.when(inner)(functools.partial(advance, turn - 2, 0))
                 begin(turn, 0)
                 theirs(turn, kept)
             else:
                 theirs(turn, range(groups))
-                for k in range(1, groups):
-                    straight_out[turn - straight, k - 1] = packed(acc[turn][lax.rem(z + k, groups)])
+                for i in range(groups - 1):
+                    t = i + (i >= z).astype(jnp.int32)
+                    k = lax.rem(t - z + groups, groups)
+                    straight_out[turn - straight, k - 1] = packed(acc[turn][t])
                     direct_copy(turn - straight, k).start()
         for b in range(bits):
-            s = turn - 2 - 4 * b
-            if 0 <= s < straight:
-                end(s, b)
-                if b + 1 < bits:
-                    begin(s, b + 1)
-                else:
-                    finish(s, acc[s][z])
+            step = functools.partial(advance, turn - 2 - 3 * b, b)
+            if swapped and b == 0 and turn < straight:
+                pl.when(jnp.logical_not(inner))(step)
+            else:
+                step()
     if straight < count:
         pltpu.make_async_remote_copy(straight_out, straight_in, di_ss, di_rs,
                                      device_id={"dp": beside}, device_id_type=MESH).wait()

time: 45.6 us -> 45.3 us (level)
  no operation moved by 1% of the time
where the time goes in v3:
time: 45.3 us; the launch traced here: 45.2 us
  Pallas kernels  44.5 us (98%)
  between operations  0.64 us (1%)
    pallas_call x1, Pallas kernels, per_device(): pl.pallas_call(functools.partial(kernel, n_dp, n_mp), out_shape=(pltpu.VM...  43.3 us
    pallas_call x1, Pallas kernels, per_device(): pl.pallas_call(write_out, out_shape=(jax.ShapeDtypeStruct(token_grads.sha...  1.21 us

profile of v3, /device:TPU:0, one launch (start us, length us, event | category | flops | bytes accessed | tf_op | source)
XLA Modules:
  0.0 45.2 jit_solution(7897592321607125822)
XLA Ops:
  0.6 43.3 %shard_map.68 = (bf16[960,512]{1,0:T(8,128)(2,1)S(1)}, f32[3,160,320]{2,1,0:T(8,128)S(1)}) custom-call(s32[8]{0:T(128)} %bitcast.5, bf16[1,2,160,512]{3,2,1,0:T(8,128)(2,1)} %bitcast.4, bf16[3,320,512]{2,1,0:T(8,128)(2,1)} %qkv_hbm.1, s32[8,64]{1,0:T(8,128)} %seg_hbm.1, bf16[320,512]{1,0:T(8,128)(2,1)} %ga_hbm.1), custom_call_target="tpu_custom_call" | custom-call | tf_op jit(solution)/shard_map/pallas_call | solution.py:426
  44.0 1.2 %shard_map.69 = (bf16[960,512]{1,0:T(8,128)(2,1)}, f32[3,160,320]{2,1,0:T(8,128)}) custom-call(bf16[960,512]{1,0:T(8,128)(2,1)S(1)} %get-tuple-element.6.tg_ref, f32[3,160,320]{2,1,0:T(8,128)S(1)} %get-tuple-element.7.wg_ref), custom_call_target="tpu_custom_call" | custom-call | tf_op jit(solution)/shard_map/pallas_call | solution.py:463

commit v4 on v3

--- a/solution.py
+++ b/solution.py
@@ -195,11 +195,11 @@
             pass_copy(q, k).start()
 
     before = min(2, chunks)
+    for q in range(before):
+        pass_on(q)
     for g in range(parts - 1):
         for k in range(1, n_dp):
             ga_copy(g, k).start()
-    for q in range(before):
-        pass_on(q)
 
     def tg_copy(s):
         at = pl.ds(*pieces[s])
@@ -343,7 +343,7 @@
     swapped = groups == 4
     inner = z == 2
     ahead = 2 if parts > 1 else 0
-    attends = {2: range(pairs // 2), 3: range(pairs // 2, pairs)} if parts > 1 else {0: range(pairs)}
+    attends = {3: range(pairs // 2), 4: range(pairs // 2, pairs)} if parts > 1 else {0: range(pairs)}
     for s in range(ahead):
         mine(s)
     members(1, far, hp_ss.at[1], hp_rs.at[1]).wait()

time: 45.3 us -> 44.9 us (level)
  no operation moved by 1% of the time
where the time goes in v4:
time: 44.9 us; the launch traced here: 44.7 us
  Pallas kernels  44.1 us (98%)
  between operations  0.64 us (1%)
    pallas_call x1, Pallas kernels, per_device(): pl.pallas_call(functools.partial(kernel, n_dp, n_mp), out_shape=(pltpu.VM...  42.9 us
    pallas_call x1, Pallas kernels, per_device(): pl.pallas_call(write_out, out_shape=(jax.ShapeDtypeStruct(token_grads.sha...  1.21 us

profile of v4, /device:TPU:0, one launch (start us, length us, event | category | flops | bytes accessed | tf_op | source)
XLA Modules:
  0.0 44.7 jit_solution(4729303547792913385)
XLA Ops:
  0.6 42.9 %shard_map.68 = (bf16[960,512]{1,0:T(8,128)(2,1)S(1)}, f32[3,160,320]{2,1,0:T(8,128)S(1)}) custom-call(s32[8]{0:T(128)} %bitcast.5, bf16[1,2,160,512]{3,2,1,0:T(8,128)(2,1)} %bitcast.4, bf16[3,320,512]{2,1,0:T(8,128)(2,1)} %qkv_hbm.1, s32[8,64]{1,0:T(8,128)} %seg_hbm.1, bf16[320,512]{1,0:T(8,128)(2,1)} %ga_hbm.1), custom_call_target="tpu_custom_call" | custom-call | tf_op jit(solution)/shard_map/pallas_call | solution.py:426
  43.5 1.2 %shard_map.69 = (bf16[960,512]{1,0:T(8,128)(2,1)}, f32[3,160,320]{2,1,0:T(8,128)}) custom-call(bf16[960,512]{1,0:T(8,128)(2,1)S(1)} %get-tuple-element.6.tg_ref, f32[3,160,320]{2,1,0:T(8,128)S(1)} %get-tuple-element.7.wg_ref), custom_call_target="tpu_custom_call" | custom-call | tf_op jit(solution)/shard_map/pallas_call | solution.py:463

commit v5 on v4

--- a/solution.py
+++ b/solution.py
@@ -161,7 +161,7 @@
         seg_copy(k).start()
     for k in range(1, far):
         hid_copy(k).start()
-    for k in range(1, n_dp):
+    for k in (*range(1, n_dp, 2), *range(2, n_dp, 2)):
         ga_copy(parts - 1, k).start()
     for q in range(chunks):
         hid_x(q).start()

time: 44.9 us -> 44.7 us (level)
  no operation moved by 1% of the time
where the time goes in v5:
time: 44.7 us; the launch traced here: 44.5 us
  Pallas kernels  43.9 us (98%)
  between operations  0.64 us (1%)
    pallas_call x1, Pallas kernels, per_device(): pl.pallas_call(functools.partial(kernel, n_dp, n_mp), out_shape=(pltpu.VM...  42.7 us
    pallas_call x1, Pallas kernels, per_device(): pl.pallas_call(write_out, out_shape=(jax.ShapeDtypeStruct(token_grads.sha...  1.21 us

profile of v5, /device:TPU:0, one launch (start us, length us, event | category | flops | bytes accessed | tf_op | source)
XLA Modules:
  0.0 44.5 jit_solution(1539982451945310119)
XLA Ops:
  0.6 42.7 %shard_map.68 = (bf16[960,512]{1,0:T(8,128)(2,1)S(1)}, f32[3,160,320]{2,1,0:T(8,128)S(1)}) custom-call(s32[8]{0:T(128)} %bitcast.5, bf16[1,2,160,512]{3,2,1,0:T(8,128)(2,1)} %bitcast.4, bf16[3,320,512]{2,1,0:T(8,128)(2,1)} %qkv_hbm.1, s32[8,64]{1,0:T(8,128)} %seg_hbm.1, bf16[320,512]{1,0:T(8,128)(2,1)} %ga_hbm.1), custom_call_target="tpu_custom_call" | custom-call | tf_op jit(solution)/shard_map/pallas_call | solution.py:426
  43.3 1.2 %shard_map.69 = (bf16[960,512]{1,0:T(8,128)(2,1)}, f32[3,160,320]{2,1,0:T(8,128)}) custom-call(bf16[960,512]{1,0:T(8,128)(2,1)S(1)} %get-tuple-element.6.tg_ref, f32[3,160,320]{2,1,0:T(8,128)S(1)} %get-tuple-element.7.wg_ref), custom_call_target="tpu_custom_call" | custom-call | tf_op jit(solution)/shard_map/pallas_call | solution.py:463

commit v6 on v5

--- a/solution.py
+++ b/solution.py
@@ -161,7 +161,7 @@
         seg_copy(k).start()
     for k in range(1, far):
         hid_copy(k).start()
-    for k in (*range(1, n_dp, 2), *range(2, n_dp, 2)):
+    for k in sorted(range(1, n_dp), key=lambda k: (1 - k % 2, -min(k, n_dp - k))):
         ga_copy(parts - 1, k).start()
     for q in range(chunks):
         hid_x(q).start()

time: 44.7 us -> 44.7 us (level)
  no operation moved by 1% of the time
where the time goes in v6:
time: 44.7 us; the launch traced here: 44.5 us
  Pallas kernels  43.9 us (98%)
  between operations  0.64 us (1%)
    pallas_call x1, Pallas kernels, per_device(): pl.pallas_call(functools.partial(kernel, n_dp, n_mp), out_shape=(pltpu.VM...  42.7 us
    pallas_call x1, Pallas kernels, per_device(): pl.pallas_call(write_out, out_shape=(jax.ShapeDtypeStruct(token_grads.sha...  1.21 us

profile of v6, /device:TPU:0, one launch (start us, length us, event | category | flops | bytes accessed | tf_op | source)
XLA Modules:
  0.0 44.5 jit_solution(3269279944433068212)
XLA Ops:
  0.6 42.7 %shard_map.68 = (bf16[960,512]{1,0:T(8,128)(2,1)S(1)}, f32[3,160,320]{2,1,0:T(8,128)S(1)}) custom-call(s32[8]{0:T(128)} %bitcast.5, bf16[1,2,160,512]{3,2,1,0:T(8,128)(2,1)} %bitcast.4, bf16[3,320,512]{2,1,0:T(8,128)(2,1)} %qkv_hbm.1, s32[8,64]{1,0:T(8,128)} %seg_hbm.1, bf16[320,512]{1,0:T(8,128)(2,1)} %ga_hbm.1), custom_call_target="tpu_custom_call" | custom-call | tf_op jit(solution)/shard_map/pallas_call | solution.py:426
  43.3 1.2 %shard_map.69 = (bf16[960,512]{1,0:T(8,128)(2,1)}, f32[3,160,320]{2,1,0:T(8,128)}) custom-call(bf16[960,512]{1,0:T(8,128)(2,1)S(1)} %get-tuple-element.6.tg_ref, f32[3,160,320]{2,1,0:T(8,128)S(1)} %get-tuple-element.7.wg_ref), custom_call_target="tpu_custom_call" | custom-call | tf_op jit(solution)/shard_map/pallas_call | solution.py:463
